TPU v7x, 32 devices: a whole 2x2x4 slice. The times are simulated.
32 devices in a mesh: prow: 2 (over core), pcol: 16 (over z, y, x).
Axes of the slice: x: 2, y: 2, z: 4, core: 2. Of those that a mesh axis runs over, the one named last changes fastest.
Arguments:
- factor_rows: float32 [8, 256, 24, 2048], P(None, 'prow', None, 'pcol'), as said below
- sensitivity: float32 [1024, 24, 2048], P('prow', None, 'pcol'), may hold values from -6 to 6
- pivots: int32 [2048], replicated, may hold values from 0 to 2047, as said below
Outputs:
- adjoint: float32 [1024, 8, 256], P(None, None, 'prow')
- updated: float32 [1024, 24, 2048], P('prow', None, 'pcol')
Inputs may be any that keep to these rules, and one draw needn't show every extreme that they name: pivots is a permutation of the first 2048 columns. `factor_rows`: in M, the entries left of each block row's diagonal block are zero and each diagonal block is lower triangular.
All inputs are finite; a program needn't handle non-finite values.
Results may differ from a plain program's by a relative error of at most 0.0001.
Values sent between devices are 32-bit elements; how exact they have to be, the bound alone decides.
No kernel may reach another device: no remote copies, remote signals or barrier semaphores. Data moves between devices by JAX's collectives and lax.ppermute only.
A program may use at most 192 MiB of HBM per device.

v0:
```python
import jax
import jax.numpy as jnp
from jax import lax
from jax.sharding import PartitionSpec as P

NB = 1024


def shards(factor_rows, sensitivity, pivots):
    pcol_count = lax.axis_size("pcol")
    row_cycles = factor_rows.shape[0]
    half_cycles = row_cycles // 2
    tile_width = factor_rows.shape[1]
    col_tiles = factor_rows.shape[2]
    local_rhs = sensitivity.shape[0]
    per_block = NB // tile_width
    pcol_index = lax.axis_index("pcol")
    tile_ids = jnp.arange(col_tiles) * pcol_count + pcol_index
    stripe_cols = pcol_count * tile_width
    gathered = lax.all_gather(sensitivity[:, :1, :], "pcol", axis=2, tiled=True)
    flat_cols = gathered.reshape(local_rhs, stripe_cols)
    swapped = jnp.take(flat_cols, pivots, axis=1)
    merged = swapped.reshape(local_rhs, 1, pcol_count, tile_width)
    own_tiles = lax.dynamic_index_in_dim(merged, pcol_index, 2, keepdims=False)
    working = jnp.concatenate([own_tiles, sensitivity[:, 1:, :]], axis=1)

    def tile_range(section):
        return (
            section * per_block // pcol_count,
            ((section + 1) * per_block - 1) // pcol_count + 1,
        )

    def solve_block(working, section):
        low_tile, high_tile = tile_range(section)
        chosen = tile_ids[low_tile:high_tile]
        inside = ((chosen >= section * per_block) & (chosen < (section + 1) * per_block)).astype(
            jnp.float32
        )
        masked = working[:, low_tile:high_tile, :] * inside[None, :, None]
        all_rhs = lax.all_gather(masked, "prow", axis=0, tiled=True)
        inverse_tiles = factor_rows[
            section * half_cycles : (section + 1) * half_cycles, :, low_tile:high_tile, :
        ]
        partial_sum = jnp.einsum(
            "hbu,atbu->hat",
            all_rhs,
            inverse_tiles,
            precision=lax.Precision.HIGHEST,
            preferred_element_type=jnp.float32,
        )
        partial_sum = partial_sum.reshape(all_rhs.shape[0], half_cycles * tile_width)
        return lax.psum(partial_sum, "pcol")

    solved_first = solve_block(working, 0)
    low_tile, high_tile = tile_range(1)
    next_tiles = high_tile - low_tile
    first_rows = factor_rows[:half_cycles, :, low_tile:high_tile, :].reshape(
        half_cycles * tile_width, next_tiles * tile_width
    )
    picked = solved_first
    early = lax.psum_scatter(
        jnp.dot(
            picked, first_rows, precision=lax.Precision.HIGHEST, preferred_element_type=jnp.float32
        ),
        "prow",
        scatter_dimension=0,
        tiled=True,
    ).reshape(local_rhs, next_tiles, tile_width)
    chosen = tile_ids[low_tile:high_tile]
    inside = ((chosen >= per_block) & (chosen < 2 * per_block)).astype(jnp.float32)
    working = working.at[:, low_tile:high_tile, :].add(-early * inside[None, :, None])
    solved_second = solve_block(working, 1)
    both_solved = jnp.concatenate([solved_first, solved_second], axis=1)
    all_rows = factor_rows.reshape(row_cycles * tile_width, col_tiles * tile_width)
    picked = both_solved
    change = lax.psum_scatter(
        jnp.dot(
            picked, all_rows, precision=lax.Precision.HIGHEST, preferred_element_type=jnp.float32
        ),
        "prow",
        scatter_dimension=0,
        tiled=True,
    ).reshape(local_rhs, col_tiles, tile_width)
    keep_cols = (tile_ids >= 2 * per_block).astype(jnp.float32)
    working = working - change * keep_cols[None, :, None]
    adjoint = jnp.concatenate([solved_first, solved_second], axis=1).reshape(
        solved_first.shape[0], row_cycles, tile_width
    )
    return (adjoint, working)


def solution(mesh):
    return jax.shard_map(
        shards,
        mesh=mesh,
        in_specs=(P(None, "prow", None, "pcol"), P("prow", None, "pcol"), P()),
        out_specs=(P(None, None, "prow"), P("prow", None, "pcol")),
        check_vma=False,
    )
```

profile of v0, /device:TPU:0, one launch (start us, length us, event | category | flops | bytes accessed | tf_op | source)
XLA Modules:
  0.0 478.7 jit_solution(9994754397476234976)
XLA Ops:
  7.2 1.7 slice.41
  8.9 0.8 copy.11
  11.4 2.5 fusion.5
  13.9 76.2 %all-gather.3.cloned.1.call-done = f32[512,1,2048]{0,2,1:T(8,128)} async-done(((f32[512,1,128]{0,2,1:T(8,128)}), f32[512,1,2048]{0,2,1:T(8,128)}) %all-gather.3.cloned.1.call-update) | async-done | bytes 4194320 | tf_op jit(solution)/shard_map/all_gather | solution.py:20
  90.2 11.7 %gather_fusion = f32[2048,512]{1,0:T(8,128)} fusion(f32[512,2048]{0,1:T(8,128)} %bitcast.40, s32[2048]{0:T(1024)S(1)} %fusion.4), kind=kCustom, calls=%fused_computation | custom fusion | bytes 8396800 | tf_op jit(solution)/shard_map/jit(_take)/gather | solution.py:22
  101.8 1.0 constant_dynamic-slice_fusion.1
  103.0 2.2 all_gather.10
  105.2 3.1 fusion.6
  108.4 124.7 %all-reduce.3.cloned.1.call-done = f32[1024,512]{1,0:T(8,128)} async-done(((f32[1024,512]{1,0:T(8,128)}), f32[1024,512]{1,0:T(8,128)}) %all-reduce.3.cloned.1.call-update) | async-done | bytes 2097168 | tf_op jit(solution)/shard_map/psum | solution.py:52
  233.0 4.2 fusion.7
  237.4 7.3 %reduce-scatter.3.cloned.1.call-done = f32[512,128]{1,0:T(8,128)} async-done(((f32[1024,128]{1,0:T(8,128)}), f32[512,128]{1,0:T(8,128)}) %reduce-scatter.3.cloned.1.call-update) | async-done | bytes 262160 | tf_op jit(solution)/shard_map/reduce_scatter | solution.py:61
  244.7 1.0 broadcast_multiply_fusion
  245.7 2.2 all-gather
  247.9 3.1 fusion.8
  251.2 1.6 constant_dynamic-update-slice_fusion.1
  252.8 125.4 %all-reduce.5.cloned.1.call-done = f32[1024,512]{1,0:T(8,128)} async-done(((f32[1024,512]{1,0:T(8,128)}), f32[1024,512]{1,0:T(8,128)}) %all-reduce.5.cloned.1.call-update) | async-done | bytes 2097168 | tf_op jit(solution)/shard_map/psum | solution.py:52
  378.3 3.2 constant_dynamic-update-slice_fusion
  381.4 60.8 %fusion = f32[1024,3072]{1,0:T(8,128)} fusion(f32[1024,1024]{1,0:T(8,128)} %constant_dynamic-update-slice_fusion, f32[128,8,24,128]{3,2,1,0:T(8,128)} %bitcast.55), kind=kOutput, calls=%fused_computation.1 | convolution fusion | flops 38654705664 | bytes 29360128 | tf_op jit(solution)/shard_map/dot_general | solution.py:77
  442.2 3.4 slice.45
  445.6 4.0 pad_maximum_fusion
  449.6 8.2 %scatter-add.4 = f32[512,24,128]{2,1,0:T(8,128)} dynamic-update-slice(f32[512,24,128]{2,1,0:T(8,128)} %pad_maximum_fusion, f32[512,1,128]{2,1,0:T(1,128)S(1)} %bitcast.52, s32[]{:T(128)} %constant.48.clone.1, s32[]{:T(128)} %constant.48.clone.1, s32[]{:T(128)} %constant.48.clone.1) | dynamic-update-slice | bytes 524292 | tf_op jit(solution)/shard_map/scatter-add | solution.py:71
  457.8 6.1 %copy.13 = f32[128,8,8,128]{3,2,1,0:T(8,128)} copy(f32[128,8,8,128]{3,1,2,0:T(8,128)} %bitcast.43) | data formatting | bytes 8388608
  464.0 4.3 copy.15
  468.6 3.6 fusion.3
  (26 shorter events, 2.4 us)
Async XLA Ops:
  7.2 83.0 %all-gather.3.cloned.1.call-start = ((), (), s32[]{:S(2)}) async-start(), calls=%async_computation.2 | async-start | bytes 4456448 | tf_op jit(solution)/shard_map/all_gather | solution.py:20
  9.8 223.2 %all-reduce.3.cloned.1.call-start = ((), (), s32[]{:S(2)}) async-start(), calls=%async_computation.3 | async-start | bytes 4194304 | tf_op jit(solution)/shard_map/psum | solution.py:52
  108.3 136.4 %reduce-scatter.3.cloned.1.call-start = ((), (), s32[]{:S(2)}) async-start(), calls=%async_computation.4 | async-start | bytes 786432 | tf_op jit(solution)/shard_map/reduce_scatter | solution.py:61
  237.2 14.0 %copy-start = (f32[1024,512]{1,0:T(8,128)S(1)}, f32[1024,512]{1,0:T(8,128)}, u32[]{:S(2)}) copy-start(f32[1024,512]{1,0:T(8,128)} %all-reduce.3.cloned.1.call-done) | copy-start | bytes 6291460
  237.2 141.0 %all-reduce.5.cloned.1.call-start = ((), (), s32[]{:S(2)}) async-start(), calls=%async_computation.5 | async-start | bytes 4194304 | tf_op jit(solution)/shard_map/psum | solution.py:52
  251.0 213.0 %reduce-scatter.5.cloned.1.call-start = ((), (), s32[]{:S(2)}) async-start(), calls=%async_computation.6 | async-start | bytes 18874368 | tf_op jit(solution)/shard_map/reduce_scatter | solution.py:76
  464.0 4.4 slice-start
  464.0 4.7 slice-start.1
Sparse Core Ops, SparseCore 0:
  11.3 78.7 all-gather.2
  108.4 124.5 all-reduce.2
  237.4 7.2 reduce-scatter.2
  251.1 127.1 all-reduce.4
  442.4 20.8 reduce-scatter.4
where the time goes:
time: 479 us
  waiting for transfers between devices  334 us (70%)
  matrix products  71.2 us (15%)
  local copies, waits for them, and re-layouts  45.1 us (9%)
  between operations  14 us (3%)
  other arithmetic  9.97 us (2%)
    psum x2, waiting for transfers between devices, solve_block(): return lax.psum(partial_sum, 'pcol')  250 us
    all_gather x1, waiting for transfers between devices, shards(): gathered = lax.all_gather(sensitivity[:, :1, :], 'pcol', axis=2, tiled=True)  76.2 us
    dot_general x1, matrix products, shards(): jnp.dot(picked, all_rows, precision=lax.Precision.HIGHEST, preferred_elem...  60.8 us
    unnamed x11, local copies, waits for them, and re-layouts  13.4 us
    gather x1, local copies, waits for them, and re-layouts, shards(): swapped = jnp.take(flat_cols, pivots, axis=1)  11.7 us
  transfers between devices with their start and end apart: 5, of which 4 were waited for; matrix products, arithmetic and copies ran while one was open for 6% of the time, Pallas kernels for 0%

commit v1 on v0

--- a/solution.py
+++ b/solution.py
@@ -17,7 +17,23 @@
     pcol_index = lax.axis_index("pcol")
     tile_ids = jnp.arange(col_tiles) * pcol_count + pcol_index
     stripe_cols = pcol_count * tile_width
-    gathered = lax.all_gather(sensitivity[:, :1, :], "pcol", axis=2, tiled=True)
+    x = sensitivity[:, :1, :]
+    ways, here, step = (lax.axis_size("pcol"), lax.axis_index("pcol"), x.shape[2])
+    lengths = [n * ways if d == 2 else n for d, n in enumerate(x.shape)]
+    gathered = lax.dynamic_update_slice_in_dim(jnp.zeros(lengths, x.dtype), x, here * step, axis=2)
+    going_up = going_down = x
+    for far in range(1, ways // 2 + 1):
+        going_up = lax.ppermute(going_up, "pcol", [(d, (d + 1) % ways) for d in range(ways)])
+        gathered = lax.dynamic_update_slice_in_dim(
+            gathered, going_up, (here - far) % ways * step, axis=2
+        )
+        if 2 * far < ways:
+            going_down = lax.ppermute(
+                going_down, "pcol", [(d, (d - 1) % ways) for d in range(ways)]
+            )
+            gathered = lax.dynamic_update_slice_in_dim(
+                gathered, going_down, (here + far) % ways * step, axis=2
+            )
     flat_cols = gathered.reshape(local_rhs, stripe_cols)
     swapped = jnp.take(flat_cols, pivots, axis=1)
     merged = swapped.reshape(local_rhs, 1, pcol_count, tile_width)

time: 479 us -> 506 us (1.056)
  starting transfers between devices: 0.39 us -> 48.9 us
  waiting for transfers between devices: 334 us -> 298 us
  local copies, waits for them, and re-layouts: 45.1 us -> 58.4 us
    all_gather x1 -> x0, waiting for transfers between devices: 76.2 us -> none  [shards(): gathered = lax.all_gather(sensitivity[:, :1, :], 'pcol', axis=2, tiled=True)]
    ppermute x0 -> x15, starting transfers between devices: none -> 48.6 us  [the longest x7 35.8 us: shards(): lax.ppermute(going_down, 'pcol', [(d, (d - 1) % ways) for d in range(ways)])]
    ppermute x0 -> x15, waiting for transfers between devices: none -> 42.9 us  [the longest x8 42.9 us: shards(): lax.ppermute(going_up, 'pcol', [(d, (d + 1) % ways) for d in range(ways)])]
    dynamic_update_slice x0 -> x16, local copies, waits for them, and re-layouts: none -> 11.5 us  [the longest x8 5.75 us: shards(): lax.dynamic_update_slice_in_dim(gathered, going_up, (here - far) % ways *...]
  transfers between devices with their start and end apart: 5 -> 19, of which waited for: 4 -> 11; matrix products, arithmetic and copies ran while one was open for 6% -> 8% of each run, Pallas kernels for 0% -> 0%
where the time goes in v1:
time: 506 us; the launch traced here: 505 us
  waiting for transfers between devices  298 us (59%)
  matrix products  71.2 us (14%)
  local copies, waits for them, and re-layouts  58.4 us (12%)
  starting transfers between devices  48.9 us (10%)
  between operations  14.3 us (3%)
  other arithmetic  9.97 us (2%)
    psum x2, waiting for transfers between devices, solve_block(): return lax.psum(partial_sum, 'pcol')  247 us
    dot_general x1, matrix products, shards(): jnp.dot(picked, all_rows, precision=lax.Precision.HIGHEST, preferred_elem...  60.8 us
    ppermute x8, waiting for transfers between devices, shards(): lax.ppermute(going_up, 'pcol', [(d, (d + 1) % ways) for d in range(ways)])  42.9 us
    ppermute x7, starting transfers between devices, shards(): lax.ppermute(going_down, 'pcol', [(d, (d - 1) % ways) for d in range(ways)])  35.8 us
    ppermute x8, starting transfers between devices, shards(): lax.ppermute(going_up, 'pcol', [(d, (d + 1) % ways) for d in range(ways)])  12.8 us
    unnamed x11, local copies, waits for them, and re-layouts  12.6 us
    gather x1, local copies, waits for them, and re-layouts, shards(): swapped = jnp.take(flat_cols, pivots, axis=1)  11.7 us
  transfers between devices with their start and end apart: 19, of which 11 were waited for; matrix products, arithmetic and copies ran while one was open for 8% of the time, Pallas kernels for 0%

profile of v1, /device:TPU:0, one launch (start us, length us, event | category | flops | bytes accessed | tf_op | source)
XLA Modules:
  0.0 504.9 jit_solution(3268297694399719007)
XLA Ops:
  9.1 7.0 %collective-permute-start.1 = (f32[512,1,128]{0,2,1:T(8,128)S(1)}, f32[512,1,128]{0,2,1:T(8,128)S(1)}, u32[]{:S(2)}, u32[]{:S(2)}) collective-permute-start(f32[512,1,128]{0,2,1:T(8,128)S(1)} %copy.11), channel_id=1, source_target_pairs={{0,15},{1,0},{2,1},{3,2},{4,3},{5,4},{6,5},{7,6},{8,7},{9,8},{10,9... | collective-permute-start | bytes 786440 | tf_op jit(solution)/shard_map/ppermute | solution.py:31
  23.7 5.6 %collective-permute-start.3 = (f32[512,1,128]{0,2,1:T(8,128)S(1)}, f32[512,1,128]{0,2,1:T(8,128)S(1)}, u32[]{:S(2)}, u32[]{:S(2)}) collective-permute-start(f32[512,1,128]{0,2,1:T(8,128)S(1)} %collective-permute-done.1), channel_id=1, source_target_pairs={{0,15},{1,0},{2,1},{3,2},{4,3},{5,4},{6,5},{7,6},{8,7},{9,8},{10,9... | collective-permute-start | bytes 786440 | tf_op jit(solution)/shard_map/ppermute | solution.py:31
  34.6 5.9 %collective-permute-start.5 = (f32[512,1,128]{0,2,1:T(8,128)S(1)}, f32[512,1,128]{0,2,1:T(8,128)S(1)}, u32[]{:S(2)}, u32[]{:S(2)}) collective-permute-start(f32[512,1,128]{0,2,1:T(8,128)S(1)} %collective-permute-done.3), channel_id=1, source_target_pairs={{0,15},{1,0},{2,1},{3,2},{4,3},{5,4},{6,5},{7,6},{8,7},{9,8},{10,9... | collective-permute-start | bytes 786440 | tf_op jit(solution)/shard_map/ppermute | solution.py:31
  40.6 4.0 collective-permute-done.2
  48.5 4.9 collective-permute-start.7
  53.4 4.2 collective-permute-done.4
  61.5 4.7 collective-permute-start.9
  66.2 4.4 collective-permute-done.6
  74.5 4.5 collective-permute-start.11
  79.0 6.4 %collective-permute-done.8 = f32[512,1,128]{0,2,1:T(8,128)S(1)} collective-permute-done((f32[512,1,128]{0,2,1:T(8,128)S(1)}, f32[512,1,128]{0,2,1:T(8,128)S(1)}, u32[]{:S(2)}, u32[]{:S(2)}) %collective-permute-start.8) | collective-permute-done | bytes 262176 | tf_op jit(solution)/shard_map/ppermute | solution.py:26
  92.5 4.8 collective-permute-done.10
  99.2 9.1 %collective-permute-done.12 = f32[512,1,128]{0,2,1:T(8,128)S(1)} collective-permute-done((f32[512,1,128]{0,2,1:T(8,128)S(1)}, f32[512,1,128]{0,2,1:T(8,128)S(1)}, u32[]{:S(2)}, u32[]{:S(2)}) %collective-permute-start.12) | collective-permute-done | bytes 262176 | tf_op jit(solution)/shard_map/ppermute | solution.py:26
  109.7 8.6 %collective-permute-done.14 = f32[512,1,128]{0,2,1:T(8,128)S(1)} collective-permute-done((f32[512,1,128]{0,2,1:T(8,128)S(1)}, f32[512,1,128]{0,2,1:T(8,128)S(1)}, u32[]{:S(2)}, u32[]{:S(2)}) %collective-permute-start.14) | collective-permute-done | bytes 262176 | tf_op jit(solution)/shard_map/ppermute | solution.py:26
  119.0 11.7 %gather_fusion = f32[2048,512]{1,0:T(8,128)} fusion(f32[512,2048]{0,1:T(8,128)} %bitcast_dynamic-update-slice_fusion, s32[2048]{0:T(1024)S(1)} %fusion.4), kind=kCustom, calls=%fused_computation | custom fusion | bytes 8396800 | tf_op jit(solution)/shard_map/jit(_take)/gather | solution.py:38
  137.2 122.0 %all-reduce.3.cloned.1.call-done = f32[1024,512]{1,0:T(8,128)} async-done(((f32[1024,512]{1,0:T(8,128)}), f32[1024,512]{1,0:T(8,128)}) %all-reduce.3.cloned.1.call-update) | async-done | bytes 2097168 | tf_op jit(solution)/shard_map/psum | solution.py:68
  259.2 4.2 fusion.7
  263.5 7.3 %reduce-scatter.3.cloned.1.call-done = f32[512,128]{1,0:T(8,128)} async-done(((f32[1024,128]{1,0:T(8,128)}), f32[512,128]{1,0:T(8,128)}) %reduce-scatter.3.cloned.1.call-update) | async-done | bytes 262160 | tf_op jit(solution)/shard_map/reduce_scatter | solution.py:77
  279.0 125.5 %all-reduce.5.cloned.1.call-done = f32[1024,512]{1,0:T(8,128)} async-done(((f32[1024,512]{1,0:T(8,128)}), f32[1024,512]{1,0:T(8,128)}) %all-reduce.5.cloned.1.call-update) | async-done | bytes 2097168 | tf_op jit(solution)/shard_map/psum | solution.py:68
  407.6 60.8 %fusion = f32[1024,3072]{1,0:T(8,128)} fusion(f32[1024,1024]{1,0:T(8,128)} %constant_dynamic-update-slice_fusion, f32[128,8,24,128]{3,2,1,0:T(8,128)} %bitcast.85), kind=kOutput, calls=%fused_computation.1 | convolution fusion | flops 38654705664 | bytes 29360128 | tf_op jit(solution)/shard_map/dot_general | solution.py:93
  471.8 4.0 pad_maximum_fusion
  475.8 8.2 %scatter-add.4 = f32[512,24,128]{2,1,0:T(8,128)} dynamic-update-slice(f32[512,24,128]{2,1,0:T(8,128)} %pad_maximum_fusion, f32[512,1,128]{2,1,0:T(1,128)S(1)} %bitcast.82, s32[]{:T(128)} %constant.150.clone.1, s32[]{:T(128)} %constant.150.clone.1, s32[]{:T(128)} %constant.150.clone.1) | dynamic-update-slice | bytes 524292 | tf_op jit(solution)/shard_map/scatter-add | solution.py:87
  484.0 6.1 %copy.13 = f32[128,8,8,128]{3,2,1,0:T(8,128)} copy(f32[128,8,8,128]{3,1,2,0:T(8,128)} %bitcast.73) | data formatting | bytes 8388608
  490.2 4.3 copy.15
  494.8 3.6 fusion.3
  (70 shorter events, 58.9 us)
Async XLA Ops:
  7.2 252.0 %all-reduce.3.cloned.1.call-start = ((), (), s32[]{:S(2)}) async-start(), calls=%async_computation.2 | async-start | bytes 4194304 | tf_op jit(solution)/shard_map/psum | solution.py:68
  9.1 14.6 %collective-permute-start.1 = (f32[512,1,128]{0,2,1:T(8,128)S(1)}, f32[512,1,128]{0,2,1:T(8,128)S(1)}, u32[]{:S(2)}, u32[]{:S(2)}) collective-permute-start(f32[512,1,128]{0,2,1:T(8,128)S(1)} %copy.11), channel_id=1, source_target_pairs={{0,15},{1,0},{2,1},{3,2},{4,3},{5,4},{6,5},{7,6},{8,7},{9,8},{10,9... | collective-permute-start | bytes 786440 | tf_op jit(solution)/shard_map/ppermute | solution.py:31
  16.1 14.7 %collective-permute-start = (f32[512,1,128]{0,2,1:T(8,128)S(1)}, f32[512,1,128]{0,2,1:T(8,128)S(1)}, u32[]{:S(2)}, u32[]{:S(2)}) collective-permute-start(f32[512,1,128]{0,2,1:T(8,128)S(1)} %copy.11), channel_id=1, source_target_pairs={{0,1},{1,2},{2,3},{3,4},{4,5},{5,6},{6,7},{7,8},{8,9},{9,10},{10,1... | collective-permute-start | bytes 786440 | tf_op jit(solution)/shard_map/ppermute | solution.py:26
  23.7 11.0 %collective-permute-start.3 = (f32[512,1,128]{0,2,1:T(8,128)S(1)}, f32[512,1,128]{0,2,1:T(8,128)S(1)}, u32[]{:S(2)}, u32[]{:S(2)}) collective-permute-start(f32[512,1,128]{0,2,1:T(8,128)S(1)} %collective-permute-done.1), channel_id=1, source_target_pairs={{0,15},{1,0},{2,1},{3,2},{4,3},{5,4},{6,5},{7,6},{8,7},{9,8},{10,9... | collective-permute-start | bytes 786440 | tf_op jit(solution)/shard_map/ppermute | solution.py:31
  30.8 13.8 %collective-permute-start.2 = (f32[512,1,128]{0,2,1:T(8,128)S(1)}, f32[512,1,128]{0,2,1:T(8,128)S(1)}, u32[]{:S(2)}, u32[]{:S(2)}) collective-permute-start(f32[512,1,128]{0,2,1:T(8,128)S(1)} %collective-permute-done), channel_id=1, source_target_pairs={{0,1},{1,2},{2,3},{3,4},{4,5},{5,6},{6,7},{7,8},{8,9},{9,10},{10,1... | collective-permute-start | bytes 786440 | tf_op jit(solution)/shard_map/ppermute | solution.py:26
  34.6 13.8 %collective-permute-start.5 = (f32[512,1,128]{0,2,1:T(8,128)S(1)}, f32[512,1,128]{0,2,1:T(8,128)S(1)}, u32[]{:S(2)}, u32[]{:S(2)}) collective-permute-start(f32[512,1,128]{0,2,1:T(8,128)S(1)} %collective-permute-done.3), channel_id=1, source_target_pairs={{0,15},{1,0},{2,1},{3,2},{4,3},{5,4},{6,5},{7,6},{8,7},{9,8},{10,9... | collective-permute-start | bytes 786440 | tf_op jit(solution)/shard_map/ppermute | solution.py:31
  44.6 13.0 %collective-permute-start.4 = (f32[512,1,128]{0,2,1:T(8,128)S(1)}, f32[512,1,128]{0,2,1:T(8,128)S(1)}, u32[]{:S(2)}, u32[]{:S(2)}) collective-permute-start(f32[512,1,128]{0,2,1:T(8,128)S(1)} %collective-permute-done.2), channel_id=1, source_target_pairs={{0,1},{1,2},{2,3},{3,4},{4,5},{5,6},{6,7},{7,8},{8,9},{9,10},{10,1... | collective-permute-start | bytes 786440 | tf_op jit(solution)/shard_map/ppermute | solution.py:26
  48.5 13.0 %collective-permute-start.7 = (f32[512,1,128]{0,2,1:T(8,128)S(1)}, f32[512,1,128]{0,2,1:T(8,128)S(1)}, u32[]{:S(2)}, u32[]{:S(2)}) collective-permute-start(f32[512,1,128]{0,2,1:T(8,128)S(1)} %collective-permute-done.5), channel_id=1, source_target_pairs={{0,15},{1,0},{2,1},{3,2},{4,3},{5,4},{6,5},{7,6},{8,7},{9,8},{10,9... | collective-permute-start | bytes 786440 | tf_op jit(solution)/shard_map/ppermute | solution.py:31
  57.5 13.0 %collective-permute-start.6 = (f32[512,1,128]{0,2,1:T(8,128)S(1)}, f32[512,1,128]{0,2,1:T(8,128)S(1)}, u32[]{:S(2)}, u32[]{:S(2)}) collective-permute-start(f32[512,1,128]{0,2,1:T(8,128)S(1)} %collective-permute-done.4), channel_id=1, source_target_pairs={{0,1},{1,2},{2,3},{3,4},{4,5},{5,6},{6,7},{7,8},{8,9},{9,10},{10,1... | collective-permute-start | bytes 786440 | tf_op jit(solution)/shard_map/ppermute | solution.py:26
  61.5 13.0 %collective-permute-start.9 = (f32[512,1,128]{0,2,1:T(8,128)S(1)}, f32[512,1,128]{0,2,1:T(8,128)S(1)}, u32[]{:S(2)}, u32[]{:S(2)}) collective-permute-start(f32[512,1,128]{0,2,1:T(8,128)S(1)} %collective-permute-done.7), channel_id=1, source_target_pairs={{0,15},{1,0},{2,1},{3,2},{4,3},{5,4},{6,5},{7,6},{8,7},{9,8},{10,9... | collective-permute-start | bytes 786440 | tf_op jit(solution)/shard_map/ppermute | solution.py:31
  70.6 14.9 %collective-permute-start.8 = (f32[512,1,128]{0,2,1:T(8,128)S(1)}, f32[512,1,128]{0,2,1:T(8,128)S(1)}, u32[]{:S(2)}, u32[]{:S(2)}) collective-permute-start(f32[512,1,128]{0,2,1:T(8,128)S(1)} %collective-permute-done.6), channel_id=1, source_target_pairs={{0,1},{1,2},{2,3},{3,4},{4,5},{5,6},{6,7},{7,8},{8,9},{9,10},{10,1... | collective-permute-start | bytes 786440 | tf_op jit(solution)/shard_map/ppermute | solution.py:26
  74.5 14.9 %collective-permute-start.11 = (f32[512,1,128]{0,2,1:T(8,128)S(1)}, f32[512,1,128]{0,2,1:T(8,128)S(1)}, u32[]{:S(2)}, u32[]{:S(2)}) collective-permute-start(f32[512,1,128]{0,2,1:T(8,128)S(1)} %collective-permute-done.9), channel_id=1, source_target_pairs={{0,15},{1,0},{2,1},{3,2},{4,3},{5,4},{6,5},{7,6},{8,7},{9,8},{10,9... | collective-permute-start | bytes 786440 | tf_op jit(solution)/shard_map/ppermute | solution.py:31
  85.4 11.9 %collective-permute-start.10 = (f32[512,1,128]{0,2,1:T(8,128)S(1)}, f32[512,1,128]{0,2,1:T(8,128)S(1)}, u32[]{:S(2)}, u32[]{:S(2)}) collective-permute-start(f32[512,1,128]{0,2,1:T(8,128)S(1)} %collective-permute-done.8), channel_id=1, source_target_pairs={{0,1},{1,2},{2,3},{3,4},{4,5},{5,6},{6,7},{7,8},{8,9},{9,10},{10,1... | collective-permute-start | bytes 786440 | tf_op jit(solution)/shard_map/ppermute | solution.py:26
  89.4 19.6 %collective-permute-start.13 = (f32[512,1,128]{0,2,1:T(8,128)S(1)}, f32[512,1,128]{0,2,1:T(8,128)S(1)}, u32[]{:S(2)}, u32[]{:S(2)}) collective-permute-start(f32[512,1,128]{0,2,1:T(8,128)S(1)} %collective-permute-done.11), channel_id=1, source_target_pairs={{0,15},{1,0},{2,1},{3,2},{4,3},{5,4},{6,5},{7,6},{8,7},{9,8},{10,9... | collective-permute-start | bytes 786440 | tf_op jit(solution)/shard_map/ppermute | solution.py:31
  97.3 10.9 %collective-permute-start.12 = (f32[512,1,128]{0,2,1:T(8,128)S(1)}, f32[512,1,128]{0,2,1:T(8,128)S(1)}, u32[]{:S(2)}, u32[]{:S(2)}) collective-permute-start(f32[512,1,128]{0,2,1:T(8,128)S(1)} %collective-permute-done.10), channel_id=1, source_target_pairs={{0,1},{1,2},{2,3},{3,4},{4,5},{5,6},{6,7},{7,8},{8,9},{9,10},{10,1... | collective-permute-start | bytes 786440 | tf_op jit(solution)/shard_map/ppermute | solution.py:26
  108.3 10.0 %collective-permute-start.14 = (f32[512,1,128]{0,2,1:T(8,128)S(1)}, f32[512,1,128]{0,2,1:T(8,128)S(1)}, u32[]{:S(2)}, u32[]{:S(2)}) collective-permute-start(f32[512,1,128]{0,2,1:T(8,128)S(1)} %collective-permute-done.12), channel_id=1, source_target_pairs={{0,1},{1,2},{2,3},{3,4},{4,5},{5,6},{6,7},{7,8},{8,9},{9,10},{10,1... | collective-permute-start | bytes 786440 | tf_op jit(solution)/shard_map/ppermute | solution.py:26
  137.2 133.7 %reduce-scatter.3.cloned.1.call-start = ((), (), s32[]{:S(2)}) async-start(), calls=%async_computation.3 | async-start | bytes 786432 | tf_op jit(solution)/shard_map/reduce_scatter | solution.py:77
  263.4 14.0 %copy-start = (f32[1024,512]{1,0:T(8,128)S(1)}, f32[1024,512]{1,0:T(8,128)}, u32[]{:S(2)}) copy-start(f32[1024,512]{1,0:T(8,128)} %all-reduce.3.cloned.1.call-done) | copy-start | bytes 6291460
  263.4 141.1 %all-reduce.5.cloned.1.call-start = ((), (), s32[]{:S(2)}) async-start(), calls=%async_computation.4 | async-start | bytes 4194304 | tf_op jit(solution)/shard_map/psum | solution.py:68
  277.2 213.0 %reduce-scatter.5.cloned.1.call-start = ((), (), s32[]{:S(2)}) async-start(), calls=%async_computation.5 | async-start | bytes 18874368 | tf_op jit(solution)/shard_map/reduce_scatter | solution.py:92
  490.2 4.4 slice-start
  490.2 4.7 slice-start.1
Sparse Core Ops, SparseCore 0:
  137.3 121.8 all-reduce.2
  263.5 7.2 reduce-scatter.2
  277.3 127.1 all-reduce.4
  468.6 20.8 reduce-scatter.4
